TPU v7x, 32 devices: a whole 2x2x4 slice. The times are simulated.
32 devices in a mesh: grp: 4 (over x, core), seq: 8 (over z, y).
Axes of the slice: x: 2, y: 2, z: 4, core: 2. Of those that a mesh axis runs over, the one named last changes fastest.
Arguments:
- cand_queries: bfloat16 [4096, 128, 128], P(('grp', 'seq')), may hold values from -256 to 256
- candidate_keys: bfloat16 [512, 128, 128], P(('grp', 'seq')), may hold values from -6 to 6
- candidate_values: bfloat16 [512, 128, 128], P(('grp', 'seq')), may hold values from -24 to 24
- prefix_rotated_keys: bfloat16 [128, 1024], P(('grp', 'seq')), may hold values from -6.1 to 6.1
- prefix_value_matrix: bfloat16 [128, 1024], P(('grp', 'seq')), may hold values from -24 to 24
- lengths: int32 [64], replicated, may hold values from 32 to 128
Outputs:
- attended: bfloat16 [4096, 128, 128], P(('grp', 'seq'))
All inputs are finite; a program needn't handle non-finite values.
Results may differ from a plain program's by a relative error of at most 0.0076.
Values may be sent and summed in bfloat16 or wider, within the bound.
No kernel may reach another device: no remote copies, remote signals or barrier semaphores. Data moves between devices by JAX's collectives and lax.ppermute only.
A program may use at most 64 MiB of HBM per device.

v0:
```python
import math
import jax
import jax.numpy as jnp
import numpy as np
from jax import lax
from jax.sharding import PartitionSpec as P

QUERY_HEADS = 64
KEY_VALUE_HEADS = 8
HEAD_WIDTH = 128
rope_base = 500000.0


def rotate(vectors, positions):
    half_width = vectors.shape[-1] // 2
    exponents = jnp.arange(half_width, dtype=jnp.float32) * (2.0 / vectors.shape[-1])
    frequency = 1.0 / jnp.power(jnp.float32(rope_base), exponents)
    angles = positions.astype(jnp.float32)[:, None] * frequency[None, :]
    cosine = jnp.cos(angles)
    sine_table = jnp.sin(angles)
    lower_half = vectors[..., :half_width]
    upper_half = vectors[..., half_width:]
    return jnp.concatenate(
        [
            lower_half * cosine - upper_half * sine_table,
            upper_half * cosine + lower_half * sine_table,
        ],
        axis=-1,
    )


def pick_heads(key_row_list, value_row_list, head_table, sequence_count):
    row_total = key_row_list.shape[0]
    stacked = jnp.stack(
        [
            key_row_list.reshape(row_total, KEY_VALUE_HEADS, HEAD_WIDTH),
            value_row_list.reshape(row_total, KEY_VALUE_HEADS, HEAD_WIDTH),
        ],
        axis=2,
    )
    picked = jnp.take(stacked, head_table, axis=1)
    return picked.reshape(row_total, sequence_count, -1).transpose(1, 0, 2)


def shards(
    cand_queries,
    candidate_keys,
    candidate_values,
    prefix_rotated_keys,
    prefix_value_matrix,
    lengths,
):
    sequence_count = lax.axis_size("seq")
    grp_count = lax.axis_size("grp")
    head_rows = cand_queries.shape[0]
    cand_length = cand_queries.shape[1]
    key_value_rows = candidate_keys.shape[0]
    group_width = QUERY_HEADS // KEY_VALUE_HEADS
    key_value_heads = min(KEY_VALUE_HEADS, key_value_rows)
    prefix_here = prefix_rotated_keys.shape[0]
    prefix_total = prefix_here * sequence_count * grp_count
    score_scale = 1.0 / math.sqrt(HEAD_WIDTH)
    prefix_pick = (
        (np.arange(sequence_count)[:, None] * key_value_rows + np.arange(key_value_heads)[None, :])
        % KEY_VALUE_HEADS
    ).reshape(-1)
    outgoing = pick_heads(prefix_rotated_keys, prefix_value_matrix, prefix_pick, sequence_count)
    spread = lax.all_to_all(outgoing, "seq", split_axis=0, concat_axis=1, tiled=True)
    prefix_pair = lax.all_gather(spread, "grp", axis=1, tiled=True)
    prefix_pair = prefix_pair.reshape(prefix_total, key_value_heads, 2, HEAD_WIDTH)
    kv_table = np.arange(key_value_rows) % key_value_heads
    prefix_key_rows = jnp.take(prefix_pair[:, :, 0], kv_table, axis=1).transpose(1, 0, 2)
    prefix_value_rows = jnp.take(prefix_pair[:, :, 1], kv_table, axis=1).transpose(1, 0, 2)
    positions = prefix_total + jnp.arange(cand_length, dtype=jnp.int32)
    new_keys = rotate(candidate_keys.astype(jnp.float32), positions).astype(jnp.bfloat16)
    rotated = rotate(cand_queries.astype(jnp.float32), positions).astype(jnp.bfloat16)
    rotated = rotated.reshape(key_value_rows, group_width * cand_length, HEAD_WIDTH)
    all_keys = jnp.concatenate([prefix_key_rows, new_keys], axis=1)
    all_values = jnp.concatenate([prefix_value_rows, candidate_values], axis=1)
    key_count = prefix_total + cand_length
    block_rows = math.gcd(key_count, 512)
    block_count = key_count // block_rows
    row_total = group_width * cand_length
    row_token = jnp.arange(row_total, dtype=jnp.int32) % cand_length
    starts = jnp.arange(block_count, dtype=jnp.int32) * block_rows

    def attend(carry, block):
        maxima, totals, weighted = carry
        block_keys, block_values, first_row = block
        scores = (
            jnp.einsum("krd,knd->krn", rotated, block_keys, preferred_element_type=jnp.float32)
            * score_scale
        )
        cand_offset = first_row + jnp.arange(block_rows, dtype=jnp.int32) - prefix_total
        scores = jnp.where((cand_offset[None, :] <= row_token[:, None])[None], scores, -jnp.inf)
        highest = jnp.maximum(maxima, jnp.max(scores, axis=-1))
        decline = jnp.exp(maxima - highest)
        exponent = jnp.exp(scores - highest[..., None])
        totals = totals * decline + jnp.sum(exponent, axis=-1)
        weighted = weighted * decline[..., None] + jnp.einsum(
            "krn,knd->krd",
            exponent.astype(jnp.bfloat16),
            block_values,
            preferred_element_type=jnp.float32,
        )
        return ((highest, totals, weighted), None)

    start_state = (
        jnp.full((key_value_rows, row_total), -1e30, jnp.float32),
        jnp.zeros((key_value_rows, row_total), jnp.float32),
        jnp.zeros((key_value_rows, row_total, HEAD_WIDTH), jnp.float32),
    )
    key_blocks = all_keys.reshape(key_value_rows, block_count, block_rows, HEAD_WIDTH).transpose(
        1, 0, 2, 3
    )
    value_blocks = all_values.reshape(
        key_value_rows, block_count, block_rows, HEAD_WIDTH
    ).transpose(1, 0, 2, 3)
    final_state, unused = lax.scan(attend, start_state, (key_blocks, value_blocks, starts))
    maxima, totals, weighted = final_state
    attended = (weighted / totals[..., None]).reshape(head_rows, cand_length, HEAD_WIDTH)
    device_place = lax.axis_index("grp") * sequence_count + lax.axis_index("seq")
    cand_of_row = (device_place * head_rows + jnp.arange(head_rows, dtype=jnp.int32)) // QUERY_HEADS
    cand_slots = jnp.arange(lengths.shape[0], dtype=jnp.int32)
    cand_limit = jnp.sum(
        jnp.where(cand_of_row[:, None] == cand_slots[None, :], lengths[None, :], 0), axis=1
    )
    visible = jnp.arange(cand_length, dtype=jnp.int32)[None, :] < cand_limit[:, None]
    return jnp.where(visible[:, :, None], attended, jnp.float32(0.0)).astype(jnp.bfloat16)


def solution(mesh):
    return jax.shard_map(
        shards,
        mesh=mesh,
        in_specs=(
            P(("grp", "seq"), None, None),
            P(("grp", "seq"), None, None),
            P(("grp", "seq"), None, None),
            P(("grp", "seq"), None),
            P(("grp", "seq"), None),
            P(),
        ),
        out_specs=P(("grp", "seq"), None, None),
        check_vma=False,
    )
```

profile of v0, /device:TPU:0, one launch (start us, length us, event | category | flops | bytes accessed | tf_op | source)
XLA Modules:
  0.0 70.8 jit_solution(9848074302536593648)
XLA Ops:
  0.0 0.7 %pad_clamp_fusion.1 = s32[1024]{0:T(1024)S(1)} fusion(s32[64]{0:T(128)} %constant.134), kind=kLoop, calls=%fused_computation.44 | loop fusion | flops 1024 | bytes 4352 | tf_op jit(solution)/shard_map/jit(_take)/gather | solution.py:41
  0.7 0.7 %pad_maximum_fusion = bf16[4,8,2,128]{3,0,2,1:T(4,128)(2,1)S(1)} fusion(bf16[4,8,1,128]{3,0,2,1:T(4,128)(2,1)} %bitcast.24, bf16[4,8,1,128]{3,0,2,1:T(4,128)(2,1)} %bitcast.25), kind=kLoop, calls=%fused_computation.41 | loop fusion | flops 8192 | bytes 32768 | tf_op jit(solution)/shard_map/stack | solution.py:34
  1.5 0.7 gather_fusion
  2.1 0.1 copy.24
  2.3 0.8 %copy.25 = bf16[8,4,2048]{2,1,0:T(4,128)(2,1)} copy(bf16[8,4,2048]{2,0,1:T(8,128)(2,1)S(1)} %bitcast.23) | data formatting | bytes 262144 | tf_op jit(solution)/shard_map/transpose | solution.py:42
  3.1 7.3 %all-to-all-start = ((bf16[8,4,2048]{2,1,0:T(4,128)(2,1)}), bf16[8,4,2048]{2,1,0:T(4,128)(2,1)S(1)}, u32[]{:S(2)}, u32[]{:S(2)}) async-start(bf16[8,4,2048]{2,1,0:T(4,128)(2,1)} %copy.25), calls=%async_computation | async-start | bytes 262144 | tf_op jit(solution)/shard_map/all_to_all | solution.py:68
  10.5 3.2 %convert_element_type.38 = f32[128,128,128]{2,1,0:T(8,128)S(1)} convert(bf16[128,128,128]{2,1,0:T(8,128)(2,1)} %param.10) | non-fusion elementwise | flops 2097152 | bytes 12582912 | tf_op jit(solution)/shard_map/convert_element_type | solution.py:76
  13.7 0.1 convert_element_type.40
  13.8 0.3 multiply_cosine_fusion
  14.2 5.0 %subtract_convert_fusion = (bf16[128,128,64]{2,1,0:T(8,128)(2,1)}, bf16[128,128,64]{2,1,0:T(8,128)(2,1)}) fusion(f32[128,128,128]{2,1,0:T(8,128)S(1)} %convert_element_type.38, f32[128,64]{1,0:T(8,128)S(1)} %get-tuple-element.39, f32[128,64]{1,0:T(8,128)S(1)} %get-tuple-element.38), kind=kLoop, calls=%fused_computation.15 | loop fusion | flops 8388608 | bytes 12648448 | tf_op jit(solution)/shard_map/convert.5
  19.2 0.4 subtract_convert_fusion.1
  19.7 0.1 select_reduce_fusion
  19.8 0.1 iota_compare_fusion
  19.9 0.2 broadcast_compare_fusion
  20.1 7.2 %all_gather.3 = bf16[1,128,2048]{2,1,0:T(8,128)(2,1)S(1)} all-gather(bf16[1,32,2048]{2,1,0:T(8,128)(2,1)S(1)} %all_to_all.10), channel_id=1, replica_groups=mesh['grp'=4,'seq'=8] {'grp'}, dimensions={1}, use_global_device_ids=true | all-gather | bytes 655360 | tf_op jit(solution)/shard_map/all_gather | solution.py:69
  27.3 0.4 reshape.191
  27.7 0.7 %fusion.31 = (bf16[128,8,1,128]{3,2,1,0:T(2,128)(2,1)S(1)}, bf16[128,8,1,128]{3,2,1,0:T(2,128)(2,1)S(1)}) fusion(bf16[128,8,2,128]{3,2,1,0:T(2,128)(2,1)S(1)} %reshape.191), kind=kLoop, calls=%fused_computation.61 | loop fusion | bytes 1048576 | tf_op jit(solution)/shard_map/slice | solution.py:73
  28.4 0.2 copy_bitcast_fusion
  28.6 0.6 gather_fusion.1
  29.3 15.3 %fusion = (f32[16,1024]{1,0:T(8,128)S(1)}, f32[16,1024,256]{1,2,0:T(8,128)}) fusion(pred[1024,256]{0,1:T(8,128)(4,1)S(1)} %broadcast_compare_fusion, bf16[16,128,64]{2,1,0:T(8,128)(2,1)S(1)} %get-tuple-element.23, bf16[16,128,64]{2,1,0:T(8,128)(2,1)S(1)} %get-tuple-element.22, bf16[16,128,128]{2,1,0:T(8,128)(2,1)S(1)} %gather_fusion.1, ...), kind=kOutput, calls=%fused_computation.5 | convolution fusion | flops 1097842688 | bytes 22347776 | tf_op jit(solution)/shard_map/while/body/eval_jaxpr/krd,knd->krn/dot_general | solution.py:91
  44.6 9.3 %fusion.1 = f32[16,1024]{1,0:T(8,128)S(1)} fusion(f32[16,1024,256]{1,2,0:T(8,128)} %get-tuple-element.41, f32[16,1024]{1,0:T(8,128)S(1)} %broadcast_maximum_fusion, pred[1024,256]{0,1:T(8,128)(4,1)S(1)} %broadcast_compare_fusion), kind=kLoop, calls=%fused_computation.6 | loop fusion | flops 16760832 | bytes 17170432 | tf_op jit(solution)/shard_map/while/body/eval_jaxpr/reduce_sum | solution.py:99
  53.9 0.6 gather_fusion.2
  54.5 11.3 %add_divide_fusion = bf16[16,1024,128]{2,1,0:T(8,128)(2,1)S(1)} fusion(f32[16,1024]{1,0:T(8,128)S(1)} %get-tuple-element.37, f32[16,1024]{1,0:T(8,128)S(1)} %get-tuple-element.36, f32[16,1024,256]{1,2,0:T(8,128)} %get-tuple-element.41, f32[16,1024]{1,0:T(8,128)S(1)} %broadcast_maximum_fusion, pred[1024,256]{0,1:T(8,128)(4,1)S(1)} %broadcast_compare_fusion, ...), kind=kOutput, calls=%fused_computation.10 | convolution fusion | flops 1098907648 | bytes 22478848 | tf_op jit(solution)/shard_map/while/body/eval_jaxpr/krn,knd->krd/dot_general | solution.py:100
  65.9 4.9 %select_convert_fusion = bf16[128,128,128]{2,1,0:T(8,128)(2,1)} fusion(bf16[128,128,128]{2,1,0:T(8,128)(2,1)S(1)} %bitcast.21, pred[128,128]{1,0:T(8,128)(4,1)S(1)} %iota_compare_fusion), kind=kLoop, calls=%fused_computation.9 | loop fusion | flops 2097152 | bytes 8404992 | tf_op jit(solution)/shard_map/convert_element_type | solution.py:129
  (19 shorter events, 0.2 us)
Async XLA Ops:
  0.0 13.7 %copy-start = (bf16[16,128,128]{2,1,0:T(8,128)(2,1)S(1)}, bf16[16,128,128]{2,1,0:T(8,128)(2,1)}, u32[]{:S(2)}) copy-start(bf16[16,128,128]{2,1,0:T(8,128)(2,1)} %param.11) | copy-start | bytes 1572868
  3.1 17.0 %all-to-all-start = ((bf16[8,4,2048]{2,1,0:T(4,128)(2,1)}), bf16[8,4,2048]{2,1,0:T(4,128)(2,1)S(1)}, u32[]{:S(2)}, u32[]{:S(2)}) async-start(bf16[8,4,2048]{2,1,0:T(4,128)(2,1)} %copy.25), calls=%async_computation | async-start | bytes 262144 | tf_op jit(solution)/shard_map/all_to_all | solution.py:68
  14.1 5.5 %copy-start.1 = (s32[16]{0:T(128)S(1)}, s32[16]{0:T(128)}, u32[]{:S(2)}) copy-start(s32[16]{0:T(128)} %constant.137) | copy-start | bytes 196
  14.2 5.5 %copy-start.3 = (s32[64]{0:T(128)S(1)}, s32[64]{0:T(128)}, u32[]{:S(2)}) copy-start(s32[64]{0:T(128)} %param.15) | copy-start | bytes 772
  44.6 10.0 %copy-start.2 = (bf16[16,128,128]{2,1,0:T(8,128)(2,1)S(1)}, bf16[16,128,128]{2,1,0:T(8,128)(2,1)}, u32[]{:S(2)}) copy-start(bf16[16,128,128]{2,1,0:T(8,128)(2,1)} %param.12) | copy-start | bytes 1572868
where the time goes:
time: 71.2 us; the launch traced here: 70.8 us
  matrix products  26.6 us (37%)
  other arithmetic  25.2 us (35%)
  starting transfers between devices  7.31 us (10%)
  blocking collectives  7.17 us (10%)
  local copies, waits for them, and re-layouts  4.28 us (6%)
    dot_general x1, matrix products, attend(): jnp.einsum('krd,knd->krn', rotated, block_keys, preferred_element_type=jn...  15.3 us
    dot_general x1, matrix products, attend(): jnp.einsum('krn,knd->krd', exponent.astype(jnp.bfloat16), block_values, p...  11.3 us
    reduce_sum x1, other arithmetic, attend(): totals = totals * decline + jnp.sum(exponent, axis=-1)  9.26 us
    all_to_all x1, starting transfers between devices, shards(): lax.all_to_all(outgoing, 'seq', split_axis=0, concat_axis=1, tiled=True)  7.31 us
    all_gather x1, blocking collectives, shards(): prefix_pair = lax.all_gather(spread, 'grp', axis=1, tiled=True)  7.17 us
    another operation x2, other arithmetic  5.46 us
    convert_element_type x1, other arithmetic, shards(): jnp.where(visible[:, :, None], attended, jnp.float32(0.0))  4.9 us
    convert_element_type x1, other arithmetic, shards(): cand_queries.astype(jnp.float32)  3.25 us
  transfers between devices with their start and end apart: 1, of which 0 were waited for; matrix products, arithmetic and copies ran while one was open for 13% of the time, Pallas kernels for 0%

commit v1 on v0

--- a/solution.py
+++ b/solution.py
@@ -66,7 +66,15 @@
     ).reshape(-1)
     outgoing = pick_heads(prefix_rotated_keys, prefix_value_matrix, prefix_pick, sequence_count)
     spread = lax.all_to_all(outgoing, "seq", split_axis=0, concat_axis=1, tiled=True)
-    prefix_pair = lax.all_gather(spread, "grp", axis=1, tiled=True)
+    n_chips = lax.axis_size("grp")
+    trail = tuple(((to_i, (to_i + 1) % n_chips) for to_i in range(n_chips)))
+    outcome_arr = [None] * n_chips
+    outcome_arr[n_chips - 1] = spread
+    for kk in range(n_chips - 2, -1, -1):
+        outcome_arr[kk] = lax.ppermute(outcome_arr[kk + 1], perm=trail, axis_name="grp")
+    local_now = jnp.concatenate(outcome_arr, 1)
+    y2 = (lax.axis_index("grp") + 1) * spread.shape[1]
+    prefix_pair = jnp.roll(local_now, y2, 1)
     prefix_pair = prefix_pair.reshape(prefix_total, key_value_heads, 2, HEAD_WIDTH)
     kv_table = np.arange(key_value_rows) % key_value_heads
     prefix_key_rows = jnp.take(prefix_pair[:, :, 0], kv_table, axis=1).transpose(1, 0, 2)

time: 71.2 us -> 83.8 us (1.18)
  waiting for transfers between devices: 0.01 us -> 12.7 us
  other arithmetic: 25.2 us -> 32.9 us
  blocking collectives: 7.17 us -> 0 us
    ppermute x0 -> x3, waiting for transfers between devices: none -> 12.7 us  [shards(): lax.ppermute(outcome_arr[kk + 1], perm=trail, axis_name='grp')]
    all_gather x1 -> x0, blocking collectives: 7.17 us -> none  [shards(): prefix_pair = lax.all_gather(spread, 'grp', axis=1, tiled=True)]
    another operation x2, other arithmetic: 5.46 us -> 9.9 us
    convert_element_type x1, other arithmetic: 3.25 us -> 6.48 us  [shards(): cand_queries.astype(jnp.float32)]
  transfers between devices with their start and end apart: 1 -> 4, of which waited for: 0 -> 3; matrix products, arithmetic and copies ran while one was open for 13% -> 21% of each run, Pallas kernels for 0% -> 0%
where the time goes in v1:
time: 83.8 us; the launch traced here: 83.4 us
  other arithmetic  32.9 us (39%)
  matrix products  26.4 us (32%)
  waiting for transfers between devices  12.7 us (15%)
  starting transfers between devices  7.37 us (9%)
  local copies, waits for them, and re-layouts  3.78 us (5%)
    dot_general x1, matrix products, attend(): jnp.einsum('krd,knd->krn', rotated, block_keys, preferred_element_type=jn...  15.1 us
    ppermute x3, waiting for transfers between devices, shards(): lax.ppermute(outcome_arr[kk + 1], perm=trail, axis_name='grp')  12.7 us
    dot_general x1, matrix products, attend(): jnp.einsum('krn,knd->krd', exponent.astype(jnp.bfloat16), block_values, p...  11.3 us
    another operation x2, other arithmetic  9.9 us
    reduce_sum x1, other arithmetic, attend(): totals = totals * decline + jnp.sum(exponent, axis=-1)  9.26 us
    all_to_all x1, starting transfers between devices, shards(): lax.all_to_all(outgoing, 'seq', split_axis=0, concat_axis=1, tiled=True)  7.31 us
    convert_element_type x1, other arithmetic, shards(): cand_queries.astype(jnp.float32)  6.48 us
    convert_element_type x1, other arithmetic, shards(): jnp.where(visible[:, :, None], attended, jnp.float32(0.0))  4.9 us
  transfers between devices with their start and end apart: 4, of which 3 were waited for; matrix products, arithmetic and copies ran while one was open for 21% of the time, Pallas kernels for 0%

profile of v1, /device:TPU:0, one launch (start us, length us, event | category | flops | bytes accessed | tf_op | source)
XLA Modules:
  0.0 83.4 jit_solution(10905010736911138128)
XLA Ops:
  0.0 0.7 pad_clamp_fusion
  0.7 0.7 pad_maximum_fusion
  1.5 0.7 gather_fusion
  2.2 0.1 copy.31
  2.4 0.8 copy.32
  3.1 7.3 %all-to-all-start = ((bf16[8,4,2048]{2,1,0:T(4,128)(2,1)}), bf16[8,4,2048]{2,1,0:T(4,128)(2,1)S(1)}, u32[]{:S(2)}, u32[]{:S(2)}) async-start(bf16[8,4,2048]{2,1,0:T(4,128)(2,1)} %copy.32), calls=%async_computation | async-start | bytes 262144 | tf_op jit(solution)/shard_map/all_to_all | solution.py:68
  10.5 6.5 %convert_element_type.38 = f32[128,128,128]{2,1,0:T(8,128)} convert(bf16[128,128,128]{2,1,0:T(8,128)(2,1)} %param.10) | non-fusion elementwise | flops 2097152 | bytes 12582912 | tf_op jit(solution)/shard_map/convert_element_type | solution.py:84
  17.0 0.1 convert_element_type.40
  17.1 0.3 multiply_cosine_fusion
  17.4 9.5 %subtract_convert_fusion = (bf16[128,128,64]{2,1,0:T(8,128)(2,1)}, bf16[128,128,64]{2,1,0:T(8,128)(2,1)}) fusion(f32[128,128,128]{2,1,0:T(8,128)} %convert_element_type.38, f32[128,64]{1,0:T(8,128)S(1)} %get-tuple-element.39, f32[128,64]{1,0:T(8,128)S(1)} %get-tuple-element.38), kind=kLoop, calls=%fused_computation.15 | loop fusion | flops 8388608 | bytes 12648448 | tf_op jit(solution)/shard_map/convert.5
  26.9 0.4 subtract_convert_fusion.1
  27.4 0.2 broadcast_compare_fusion
  27.6 4.2 %collective-permute-done = bf16[1,32,2048]{2,1,0:T(8,128)(2,1)S(1)} collective-permute-done((bf16[1,32,2048]{2,1,0:T(8,128)(2,1)S(1)}, bf16[1,32,2048]{2,1,0:T(8,128)(2,1)S(1)}, u32[]{:S(2)}, u32[]{:S(2)}) %collective-permute-start) | collective-permute-done | bytes 131104 | tf_op jit(solution)/shard_map/ppermute | solution.py:74
  31.9 4.3 %collective-permute-done.1 = bf16[1,32,2048]{2,1,0:T(8,128)(2,1)S(1)} collective-permute-done((bf16[1,32,2048]{2,1,0:T(8,128)(2,1)S(1)}, bf16[1,32,2048]{2,1,0:T(8,128)(2,1)S(1)}, u32[]{:S(2)}, u32[]{:S(2)}) %collective-permute-start.1) | collective-permute-done | bytes 131104 | tf_op jit(solution)/shard_map/ppermute | solution.py:74
  36.3 4.3 %collective-permute-done.2 = bf16[1,32,2048]{2,1,0:T(8,128)(2,1)S(1)} collective-permute-done((bf16[1,32,2048]{2,1,0:T(8,128)(2,1)S(1)}, bf16[1,32,2048]{2,1,0:T(8,128)(2,1)S(1)}, u32[]{:S(2)}, u32[]{:S(2)}) %collective-permute-start.2) | collective-permute-done | bytes 131104 | tf_op jit(solution)/shard_map/ppermute | solution.py:74
  40.8 0.3 copy.33
  41.1 0.2 copy.35
  41.3 0.7 gather_fusion.1
  42.0 15.1 %fusion = (f32[16,1024]{1,0:T(8,128)S(1)}, f32[16,1024,256]{1,2,0:T(8,128)}) fusion(pred[1024,256]{0,1:T(8,128)(4,1)S(1)} %broadcast_compare_fusion, bf16[16,128,64]{2,1,0:T(8,128)(2,1)S(1)} %get-tuple-element.23, bf16[16,128,64]{2,1,0:T(8,128)(2,1)S(1)} %get-tuple-element.22, bf16[16,128,128]{2,1,0:T(8,128)(2,1)S(1)} %gather_fusion.1, ...), kind=kOutput, calls=%fused_computation.5 | convolution fusion | flops 1097842688 | bytes 22347776 | tf_op jit(solution)/shard_map/while/body/eval_jaxpr/krd,knd->krn/dot_general | solution.py:99
  57.0 9.3 %fusion.1 = f32[16,1024]{1,0:T(8,128)S(1)} fusion(f32[16,1024,256]{1,2,0:T(8,128)} %get-tuple-element.41, f32[16,1024]{1,0:T(8,128)S(1)} %broadcast_maximum_fusion, pred[1024,256]{0,1:T(8,128)(4,1)S(1)} %broadcast_compare_fusion), kind=kLoop, calls=%fused_computation.6 | loop fusion | flops 16760832 | bytes 17170432 | tf_op jit(solution)/shard_map/while/body/eval_jaxpr/reduce_sum | solution.py:107
  66.3 0.2 copy.37
  66.5 0.7 gather_fusion.2
  67.2 11.3 %add_divide_fusion = bf16[16,1024,128]{2,1,0:T(8,128)(2,1)S(1)} fusion(f32[16,1024]{1,0:T(8,128)S(1)} %get-tuple-element.37, f32[16,1024]{1,0:T(8,128)S(1)} %get-tuple-element.36, f32[16,1024,256]{1,2,0:T(8,128)} %get-tuple-element.41, f32[16,1024]{1,0:T(8,128)S(1)} %broadcast_maximum_fusion, pred[1024,256]{0,1:T(8,128)(4,1)S(1)} %broadcast_compare_fusion, ...), kind=kOutput, calls=%fused_computation.10 | convolution fusion | flops 1098907648 | bytes 22478848 | tf_op jit(solution)/shard_map/while/body/eval_jaxpr/krn,knd->krd/dot_general | solution.py:108
  78.5 4.9 %select_convert_fusion = bf16[128,128,128]{2,1,0:T(8,128)(2,1)} fusion(bf16[128,128,128]{2,1,0:T(8,128)(2,1)S(1)} %bitcast.20, pred[128,128]{1,0:T(8,128)(4,1)S(1)} %iota_compare_fusion), kind=kLoop, calls=%fused_computation.9 | loop fusion | flops 2097152 | bytes 8404992 | tf_op jit(solution)/shard_map/convert_element_type | solution.py:137
  (31 shorter events, 0.6 us)
Async XLA Ops:
  0.0 17.0 %copy-start = (bf16[16,128,128]{2,1,0:T(8,128)(2,1)S(1)}, bf16[16,128,128]{2,1,0:T(8,128)(2,1)}, u32[]{:S(2)}) copy-start(bf16[16,128,128]{2,1,0:T(8,128)(2,1)} %param.11) | copy-start | bytes 1572868
  3.1 24.2 %all-to-all-start = ((bf16[8,4,2048]{2,1,0:T(4,128)(2,1)}), bf16[8,4,2048]{2,1,0:T(4,128)(2,1)S(1)}, u32[]{:S(2)}, u32[]{:S(2)}) async-start(bf16[8,4,2048]{2,1,0:T(4,128)(2,1)} %copy.32), calls=%async_computation | async-start | bytes 262144 | tf_op jit(solution)/shard_map/all_to_all | solution.py:68
  17.4 14.4 %copy-start.2 = (s32[64]{0:T(128)S(1)}, s32[64]{0:T(128)}, u32[]{:S(2)}) copy-start(s32[64]{0:T(128)} %param.15) | copy-start | bytes 772
  27.4 4.4 %collective-permute-start = (bf16[1,32,2048]{2,1,0:T(8,128)(2,1)S(1)}, bf16[1,32,2048]{2,1,0:T(8,128)(2,1)S(1)}, u32[]{:S(2)}, u32[]{:S(2)}) collective-permute-start(bf16[1,32,2048]{2,1,0:T(8,128)(2,1)S(1)} %all_to_all.10), channel_id=1, source_target_pairs={{0,8},{8,16},{16,24},{24,0},{1,9},{9,17},{17,25},{25,1},{2,10},{10... | collective-permute-start | bytes 393224 | tf_op jit(solution)/shard_map/ppermute | solution.py:74
  31.8 4.4 %collective-permute-start.1 = (bf16[1,32,2048]{2,1,0:T(8,128)(2,1)S(1)}, bf16[1,32,2048]{2,1,0:T(8,128)(2,1)S(1)}, u32[]{:S(2)}, u32[]{:S(2)}) collective-permute-start(bf16[1,32,2048]{2,1,0:T(8,128)(2,1)S(1)} %collective-permute-done), channel_id=1, source_target_pairs={{0,8},{8,16},{16,24},{24,0},{1,9},{9,17},{17,25},{25,1},{2,10},{10... | collective-permute-start | bytes 393224 | tf_op jit(solution)/shard_map/ppermute | solution.py:74
  36.2 4.4 %collective-permute-start.2 = (bf16[1,32,2048]{2,1,0:T(8,128)(2,1)S(1)}, bf16[1,32,2048]{2,1,0:T(8,128)(2,1)S(1)}, u32[]{:S(2)}, u32[]{:S(2)}) collective-permute-start(bf16[1,32,2048]{2,1,0:T(8,128)(2,1)S(1)} %collective-permute-done.1), channel_id=1, source_target_pairs={{0,8},{8,16},{16,24},{24,0},{1,9},{9,17},{17,25},{25,1},{2,10},{10... | collective-permute-start | bytes 393224 | tf_op jit(solution)/shard_map/ppermute | solution.py:74
  57.0 10.2 %copy-start.1 = (bf16[16,128,128]{2,1,0:T(8,128)(2,1)S(1)}, bf16[16,128,128]{2,1,0:T(8,128)(2,1)}, u32[]{:S(2)}) copy-start(bf16[16,128,128]{2,1,0:T(8,128)(2,1)} %param.12) | copy-start | bytes 1572868
